TPU v7x, 512 devices: a whole 4x4x16 slice. The times are simulated.
512 devices in a mesh: ctx: 64 (over y_hi, z, core), dp: 8 (over x, y_lo).
Axes of the slice: x: 4, y: 4 (y_hi: 2, y_lo: 2; y = y_hi * 2 + y_lo), z: 16, core: 2. Of those that a mesh axis runs over, the one named last changes fastest.
Arguments:
- queries: bfloat16 [8192, 2048], P('ctx', 'dp')
- keys: bfloat16 [8192, 2048], P('ctx', 'dp')
- values: bfloat16 [8192, 2048], P('ctx', 'dp'), may hold values from -6 to 6
- old_keys: bfloat16 [2048, 2048], P('ctx', 'dp'), may hold values from -6 to 6
- old_values: bfloat16 [2048, 2048], P('ctx', 'dp'), may hold values from -6 to 6
- conv_keys: bfloat16 [16, 4, 128, 128], P('dp'), may hold values from -0.25 to 0.25
- conv_values: bfloat16 [16, 4, 128, 128], P('dp'), may hold values from -0.25 to 0.25
- out_proj: bfloat16 [4096, 2048], P('ctx', 'dp'), may hold values from -0.125 to 0.125
- residual: bfloat16 [8192, 4096], P('ctx', 'dp'), may hold values from -4 to 4
- gain: bfloat16 [4096], P('dp'), may hold values from 0.5 to 1.5
- span_order: int32 [128], P('ctx'), may hold values from 0 to 127, as said below
- memory_length: int32 [1], replicated, may hold values from 128 to 512
Outputs:
- layer_out: bfloat16 [8192, 4096], P('ctx', 'dp')
Inputs may be any that keep to these rules, and one draw needn't show every extreme that they name: `span_order`: entries 2 i and 2 i + 1 are blocks c and 127 - c for some c, in either order; every block appears once. `memory_length`: the valid slots are the last ones.
All inputs are finite; a program needn't handle non-finite values.
Results may differ from a plain program's by a relative error of at most 0.018.
Values may be sent and summed in bfloat16 or wider, within the bound.
A program may use at most 64 MiB of HBM per device.

v0:
```python
import math
import jax
import jax.numpy as jnp
from jax import lax
from jax.sharding import PartitionSpec as P

neg_big = -1e30


def compress(old, conv_weight):
    slots = old.shape[0] // 4
    groups = conv_weight.shape[0]
    width = conv_weight.shape[2]
    grouped = old.reshape(slots, 4, groups, width)
    mixed = jnp.einsum("jthc,htce->jhe", grouped, conv_weight, preferred_element_type=jnp.float32)
    return mixed.reshape(slots, groups * width).astype(jnp.bfloat16)


def attend(carry, queries3, key_rows, value_rows, allowed, scale):
    run_max, run_sum, run_acc = carry
    rows = key_rows.shape[0]
    groups = queries3.shape[1]
    width = queries3.shape[2]
    keys3 = key_rows.reshape(rows, groups, width)
    values3 = value_rows.reshape(rows, groups, width)
    scores = jnp.einsum("thd,rhd->htr", queries3, keys3, preferred_element_type=jnp.float32) * scale
    scores = jnp.where(allowed[None], scores, neg_big)
    new_max = jnp.maximum(run_max, jnp.max(scores, axis=2))
    weights = jnp.where(allowed[None], jnp.exp(scores - new_max[:, :, None]), 0.0)
    factor = jnp.exp(run_max - new_max)
    new_sum = run_sum * factor + jnp.sum(weights, axis=2)
    update = jnp.einsum(
        "htr,rhd->htd", weights.astype(jnp.bfloat16), values3, preferred_element_type=jnp.float32
    )
    return (new_max, new_sum, run_acc * factor[:, :, None] + update)


def local(
    queries,
    keys,
    values,
    old_keys,
    old_values,
    conv_keys,
    conv_values,
    out_proj,
    residual,
    gain,
    span_order,
    memory_length,
):
    tok_rows = queries.shape[0]
    groups = conv_keys.shape[0]
    width = conv_keys.shape[2]
    half_rows = tok_rows // 2
    scale = 1.0 / math.sqrt(width)
    ctx_count = lax.axis_size("ctx")
    gain_f = gain.astype(jnp.float32)[None, :]
    offsets = jnp.arange(half_rows, dtype=jnp.int32)
    query_pos = (span_order[:, None] * half_rows + offsets[None, :]).reshape(tok_rows)
    queries3 = queries.reshape(tok_rows, groups, width)
    table = lax.all_gather(span_order, "ctx", axis=0, tiled=True)
    slot_count = old_keys.shape[0] // 4 * ctx_count
    first_valid = slot_count - memory_length[0]
    start_carry = (
        jnp.full((groups, tok_rows), neg_big, jnp.float32),
        jnp.zeros((groups, tok_rows), jnp.float32),
        jnp.zeros((groups, tok_rows, width), jnp.float32),
    )
    whole_keys, whole_values = (
        lax.all_gather(old_keys, "ctx", axis=0, tiled=True),
        lax.all_gather(old_values, "ctx", axis=0, tiled=True),
    )
    mem_keys = compress(whole_keys, conv_keys)
    mem_values = compress(whole_values, conv_values)
    slot_index = jnp.arange(slot_count, dtype=jnp.int32)
    visible = jnp.broadcast_to((slot_index >= first_valid)[None, :], (tok_rows, slot_count))
    carry = attend(start_carry, queries3, mem_keys, mem_values, visible, scale)
    span_ids = jnp.arange(table.shape[0], dtype=jnp.int32)
    pieces = (
        lax.all_gather(keys, "ctx", axis=0, tiled=True),
        lax.all_gather(values, "ctx", axis=0, tiled=True),
    )
    rows = pieces[0].shape[0]
    index = jnp.arange(rows, dtype=jnp.int32)
    slot_span = index // half_rows
    picked = jnp.sum(jnp.where(slot_span[:, None] == span_ids[None, :], table[None, :], 0), axis=1)
    key_pos = picked * half_rows + index % half_rows
    visible = key_pos[None, :] <= query_pos[:, None]
    run_max, run_sum, run_acc = attend(carry, queries3, pieces[0], pieces[1], visible, scale)
    attn = (
        (run_acc / run_sum[:, :, None])
        .transpose(1, 0, 2)
        .reshape(tok_rows, groups * width)
        .astype(jnp.bfloat16)
    )
    partial_sums = lax.dot_general(
        attn,
        lax.all_gather(out_proj, "ctx", axis=0, tiled=True),
        (((1,), (1,)), ((), ())),
        preferred_element_type=jnp.float32,
    )
    features = partial_sums.shape[1]
    share = lax.psum_scatter(
        partial_sums.astype(jnp.bfloat16), "dp", scatter_dimension=1, tiled=True
    ).astype(jnp.float32)
    stream = residual.astype(jnp.float32) + share
    power = lax.psum(jnp.sum(stream * stream, axis=1), "dp") / features
    normed = stream * lax.rsqrt(power + 1e-06)[:, None] * gain_f
    return normed.astype(jnp.bfloat16)


def solution(mesh):
    placed = (
        P("ctx", "dp"),
        P("ctx", "dp"),
        P("ctx", "dp"),
        P("ctx", "dp"),
        P("ctx", "dp"),
        P("dp", None, None, None),
        P("dp", None, None, None),
        P("ctx", "dp"),
        P("ctx", "dp"),
        P("dp"),
        P("ctx"),
        P(),
    )
    return jax.shard_map(
        local, mesh=mesh, in_specs=placed, out_specs=P("ctx", "dp"), check_vma=False
    )
```

profile of v0, /device:TPU:16, one launch (start us, length us, event | category | flops | bytes accessed | tf_op | source)
XLA Modules:
  0.0 803.5 jit_solution(13249138557412104678)
XLA Ops:
  6.5 0.7 all-gather.6.cloned.1.call-update
  7.3 0.7 all-gather.8.cloned.1.call-update
  8.1 0.7 all-gather.12.cloned.1.call-update
  8.8 1.6 copy.39
  10.4 0.5 all-gather.14.cloned.1.call-update
  11.0 0.7 broadcast_multiply_fusion
  11.7 1.3 dynamic-slice
  13.6 0.9 dynamic-update-slice
  14.5 28.8 %all-reduce = s32[128]{0:T(128)S(1)} all-reduce(s32[128]{0:T(128)S(1)} %dynamic-update-slice), channel_id=1, replica_groups=mesh['ctx'=64,'dp'=8] {'ctx'}, use_global_device_ids=true, to_apply=%add | all-reduce | flops 128 | bytes 1024
  43.3 2.5 select_reduce_fusion
  45.9 0.1 iota_add_fusion
  46.0 0.1 add.85
  46.0 0.6 broadcast_compare_fusion
  47.4 106.9 %all-gather.6.cloned.1.call-done = bf16[2048,256]{1,0:T(8,128)(2,1)} async-done(((bf16[32,256]{1,0:T(8,128)(2,1)}), bf16[2048,256]{1,0:T(8,128)(2,1)}) %all-gather.6.cloned.1.call-update) | async-done | bytes 1048592 | tf_op jit(solution)/shard_map/all_gather | solution.py:71
  154.2 1.3 reshape.125
  155.6 138.6 %all-gather.8.cloned.1.call-done = bf16[2048,256]{1,0:T(8,128)(2,1)} async-done(((bf16[32,256]{1,0:T(8,128)(2,1)}), bf16[2048,256]{1,0:T(8,128)(2,1)}) %all-gather.8.cloned.1.call-update) | async-done | bytes 1048592 | tf_op jit(solution)/shard_map/all_gather | solution.py:72
  294.2 1.3 reshape.127
  295.6 1.6 fusion.54
  297.1 146.2 %all-gather.12.cloned.1.call-done = bf16[8192,256]{1,0:T(8,128)(2,1)} async-done(((bf16[128,256]{1,0:T(8,128)(2,1)}), bf16[8192,256]{1,0:T(8,128)(2,1)}) %all-gather.12.cloned.1.call-update) | async-done | bytes 4194320 | tf_op jit(solution)/shard_map/all_gather | solution.py:82
  443.3 6.4 copy.42
  449.8 138.0 %all-gather.10.cloned.1.call-done = bf16[8192,256]{0,1:T(8,128)(2,1)} async-done(((bf16[128,256]{0,1:T(8,128)(2,1)}), bf16[8192,256]{0,1:T(8,128)(2,1)}) %all-gather.10.cloned.1.call-update) | async-done | bytes 4194320 | tf_op jit(solution)/shard_map/all_gather | solution.py:81
  587.8 4.6 fusion.57
  592.5 0.2 fusion.28
  592.6 2.1 fusion.1
  594.8 1.8 fusion.15
  596.6 0.6 fusion.23
  597.3 131.5 %all-gather.14.cloned.1.call-done = bf16[4096,256]{1,0:T(8,128)(2,1)} async-done(((bf16[64,256]{1,0:T(8,128)(2,1)}), bf16[4096,256]{1,0:T(8,128)(2,1)}) %all-gather.14.cloned.1.call-update) | async-done | bytes 2097168 | tf_op jit(solution)/shard_map/all_gather | solution.py:99
  728.7 3.4 convolution_convert_fusion
  732.2 44.4 %reduce-scatter.2.cloned.1.call-done = bf16[128,512]{1,0:T(8,128)(2,1)} async-done(((bf16[128,4096]{1,0:T(8,128)(2,1)}), bf16[128,512]{1,0:T(8,128)(2,1)}) %reduce-scatter.2.cloned.1.call-update) | async-done | bytes 131088 | tf_op jit(solution)/shard_map/reduce_scatter | solution.py:104
  776.5 1.0 multiply_reduce_fusion
  777.6 17.5 %psum.7 = f32[128]{0:T(128)S(1)} all-reduce(f32[128]{0:T(128)S(1)} %multiply_reduce_fusion), channel_id=1, replica_groups=mesh['ctx'=64,'dp'=8] {'dp'}, use_global_device_ids=true, to_apply=%region_7.8 | all-reduce | flops 128 | bytes 1024 | tf_op jit(solution)/shard_map/psum | solution.py:108
  795.0 1.7 multiply_convert_fusion
  (30 shorter events, 0.3 us)
Async XLA Ops:
  6.5 289.0 %copy-start = (bf16[2,4,128,128]{3,2,1,0:T(8,128)(2,1)S(1)}, bf16[2,4,128,128]{3,2,1,0:T(8,128)(2,1)}, u32[]{:S(2)}) copy-start(bf16[2,4,128,128]{3,2,1,0:T(8,128)(2,1)} %param.17) | copy-start | bytes 786436
  6.5 289.0 %copy-start.4 = (bf16[128,256]{1,0:T(8,128)(2,1)S(1)}, bf16[128,256]{1,0:T(8,128)(2,1)}, u32[]{:S(2)}) copy-start(bf16[128,256]{1,0:T(8,128)(2,1)} %param.12) | copy-start | bytes 196612
  6.5 147.7 %all-gather.6.cloned.1.call-start = ((), (), s32[]{:S(2)}) async-start(), calls=%async_computation.1 | async-start | bytes 1064960 | tf_op jit(solution)/shard_map/all_gather | solution.py:71
  7.3 286.9 %all-gather.8.cloned.1.call-start = ((), (), s32[]{:S(2)}) async-start(), calls=%async_computation.2 | async-start | bytes 1064960 | tf_op jit(solution)/shard_map/all_gather | solution.py:72
  8.0 435.3 %all-gather.12.cloned.1.call-start = ((), (), s32[]{:S(2)}) async-start(), calls=%async_computation.4 | async-start | bytes 4259840 | tf_op jit(solution)/shard_map/all_gather | solution.py:82
  8.7 579.0 %all-gather.10.cloned.1.call-start = ((), (), s32[]{:S(2)}) async-start(), calls=%async_computation.3 | async-start | bytes 4259840 | tf_op jit(solution)/shard_map/all_gather | solution.py:81
  10.4 718.3 %all-gather.14.cloned.1.call-start = ((), (), s32[]{:S(2)}) async-start(), calls=%async_computation.5 | async-start | bytes 2129920 | tf_op jit(solution)/shard_map/all_gather | solution.py:99
  11.0 765.6 %reduce-scatter.2.cloned.1.call-start = ((), (), s32[]{:S(2)}) async-start(), calls=%async_computation.6 | async-start | bytes 1179648 | tf_op jit(solution)/shard_map/reduce_scatter | solution.py:104
  587.8 4.7 copy-start.2
  592.6 2.2 copy-start.1
  594.8 1.8 copy-start.6
  596.6 135.5 %copy-start.5 = (bf16[512]{0:T(512)(128)(2,1)S(1)}, bf16[512]{0:T(512)(128)(2,1)}, u32[]{:S(2)}) copy-start(bf16[512]{0:T(512)(128)(2,1)} %param.21) | copy-start | bytes 3076
  596.6 179.9 %copy-start.3 = (bf16[128,512]{1,0:T(8,128)(2,1)S(1)}, bf16[128,512]{1,0:T(8,128)(2,1)}, u32[]{:S(2)}) copy-start(bf16[128,512]{1,0:T(8,128)(2,1)} %param.20) | copy-start | bytes 393220
Sparse Core Ops, SparseCore 0:
  10.6 143.5 all-gather.5
  157.5 136.6 all-gather.7
  297.5 145.7 all-gather.11
  446.2 141.5 all-gather.9
  590.9 137.7 all-gather.13
  732.3 44.2 reduce-scatter.1
where the time goes:
time: 804 us
  waiting for transfers between devices  708 us (88%)
  blocking collectives  46.3 us (6%)
  between operations  14.9 us (2%)
  local copies, waits for them, and re-layouts  13 us (2%)
  matrix products  12 us (1%)
  other arithmetic  8.94 us (1%)
    all_gather x1, waiting for transfers between devices, local(): lax.all_gather(values, 'ctx', axis=0, tiled=True)  146 us
    all_gather x1, waiting for transfers between devices, local(): lax.all_gather(old_values, 'ctx', axis=0, tiled=True)  139 us
    all_gather x1, waiting for transfers between devices, local(): lax.all_gather(keys, 'ctx', axis=0, tiled=True)  138 us
    all_gather x1, waiting for transfers between devices, local(): lax.all_gather(out_proj, 'ctx', axis=0, tiled=True)  131 us
    all_gather x1, waiting for transfers between devices, local(): lax.all_gather(old_keys, 'ctx', axis=0, tiled=True)  107 us
    reduce_scatter x1, waiting for transfers between devices, local(): lax.psum_scatter(partial_sums.astype(jnp.bfloat16), 'dp', scatter_dimensi...  44.4 us
    unnamed x1, blocking collectives  28.8 us
    psum x1, blocking collectives, local(): power = lax.psum(jnp.sum(stream * stream, axis=1), 'dp') / features  17.5 us
  transfers between devices with their start and end apart: 6, of which 6 were waited for; matrix products, arithmetic and copies ran while one was open for 3% of the time, Pallas kernels for 0%

commit v1 on v0

--- a/solution.py
+++ b/solution.py
@@ -3,6 +3,7 @@
 import jax.numpy as jnp
 from jax import lax
 from jax.sharding import PartitionSpec as P
+from jax.lax import all_to_all, axis_size
 
 neg_big = -1e30
 
@@ -94,9 +95,16 @@
         .reshape(tok_rows, groups * width)
         .astype(jnp.bfloat16)
     )
+
+    def _guide_widths(axis_no, u_in, axis_id):
+        moved = jnp.stack([u_in for _ in range(axis_size(axis_id))])
+        part_next = all_to_all(moved, axis_id, 0, 0)
+        y1 = jnp.concatenate(part_next, axis=axis_no)
+        return y1
+
     partial_sums = lax.dot_general(
         attn,
-        lax.all_gather(out_proj, "ctx", axis=0, tiled=True),
+        _guide_widths(0, out_proj, "ctx"),
         (((1,), (1,)), ((), ())),
         preferred_element_type=jnp.float32,
     )

time: 804 us -> 679 us (0.84)
  waiting for transfers between devices: 708 us -> 481 us
  blocking collectives: 46.3 us -> 125 us
  starting transfers between devices: 0.2 us -> 19 us
    all_gather x1 -> x0, waiting for transfers between devices: 131 us -> none  [local(): lax.all_gather(out_proj, 'ctx', axis=0, tiled=True)]
    all_gather x1, waiting for transfers between devices: 107 us -> 15.8 us  [local(): lax.all_gather(old_keys, 'ctx', axis=0, tiled=True)]
    unnamed x1, blocking collectives: 28.8 us -> 108 us
    all_to_all x0 -> x1, starting transfers between devices: none -> 18.8 us  [_guide_widths(): part_next = all_to_all(moved, axis_id, 0, 0)]
  transfers between devices with their start and end apart: 6 -> 6, of which waited for: 6 -> 5; matrix products, arithmetic and copies ran while one was open for 3% -> 5% of each run, Pallas kernels for 0% -> 0%
where the time goes in v1:
time: 679 us; the launch traced here: 678 us
  waiting for transfers between devices  481 us (71%)
  blocking collectives  125 us (18%)
  starting transfers between devices  19 us (3%)
  local copies, waits for them, and re-layouts  16.3 us (2%)
  between operations  14.6 us (2%)
  matrix products  13.7 us (2%)
  other arithmetic  8.3 us (1%)
    all_gather x1, waiting for transfers between devices, local(): lax.all_gather(values, 'ctx', axis=0, tiled=True)  144 us
    all_gather x1, waiting for transfers between devices, local(): lax.all_gather(keys, 'ctx', axis=0, tiled=True)  138 us
    all_gather x1, waiting for transfers between devices, local(): lax.all_gather(old_values, 'ctx', axis=0, tiled=True)  137 us
    unnamed x1, blocking collectives  108 us
    reduce_scatter x1, waiting for transfers between devices, local(): lax.psum_scatter(partial_sums.astype(jnp.bfloat16), 'dp', scatter_dimensi...  43.7 us
    all_to_all x1, starting transfers between devices, _guide_widths(): part_next = all_to_all(moved, axis_id, 0, 0)  18.8 us
    psum x1, blocking collectives, local(): power = lax.psum(jnp.sum(stream * stream, axis=1), 'dp') / features  17.5 us
    all_gather x1, waiting for transfers between devices, local(): lax.all_gather(old_keys, 'ctx', axis=0, tiled=True)  15.8 us
  transfers between devices with their start and end apart: 6, of which 5 were waited for; matrix products, arithmetic and copies ran while one was open for 5% of the time, Pallas kernels for 0%

profile of v1, /device:TPU:16, one launch (start us, length us, event | category | flops | bytes accessed | tf_op | source)
XLA Modules:
  0.0 678.2 jit_solution(11304450260173666970)
XLA Ops:
  6.5 0.7 all-gather.5.cloned.1.call-update
  7.3 0.7 all-gather.7.cloned.1.call-update
  8.1 0.7 all-gather.11.cloned.1.call-update
  8.8 1.6 copy.39
  10.4 2.3 stack.2
  12.7 18.8 %all-to-all-start = ((bf16[64,64,256]{2,1,0:T(8,128)(2,1)}), bf16[64,64,256]{2,1,0:T(8,128)(2,1)S(1)}, u32[]{:S(2)}, u32[]{:S(2)}) async-start(bf16[64,64,256]{2,1,0:T(8,128)(2,1)} %stack.2), calls=%async_computation | async-start | bytes 4194304 | tf_op jit(solution)/shard_map/all_to_all | solution.py:101
  31.6 0.0 reduce-scatter.2.cloned.1.call-start
  31.7 0.1 iota_add_fusion
  31.7 0.1 add.85
  32.5 1.3 dynamic-slice
  34.5 0.2 dynamic-update-slice
  34.7 107.6 %all-reduce = s32[128]{0:T(128)S(1)} all-reduce(s32[128]{0:T(128)S(1)} %dynamic-update-slice), channel_id=1, replica_groups=mesh['ctx'=64,'dp'=8] {'ctx'}, use_global_device_ids=true, to_apply=%add | all-reduce | flops 128 | bytes 1024
  142.3 2.5 select_reduce_fusion
  144.9 0.6 broadcast_compare_fusion
  145.5 15.8 %all-gather.5.cloned.1.call-done = bf16[2048,256]{1,0:T(8,128)(2,1)} async-done(((bf16[32,256]{1,0:T(8,128)(2,1)}), bf16[2048,256]{1,0:T(8,128)(2,1)}) %all-gather.5.cloned.1.call-update) | async-done | bytes 1048592 | tf_op jit(solution)/shard_map/all_gather | solution.py:72
  161.3 2.1 reshape.130
  163.5 137.3 %all-gather.7.cloned.1.call-done = bf16[2048,256]{1,0:T(8,128)(2,1)} async-done(((bf16[32,256]{1,0:T(8,128)(2,1)}), bf16[2048,256]{1,0:T(8,128)(2,1)}) %all-gather.7.cloned.1.call-update) | async-done | bytes 1048592 | tf_op jit(solution)/shard_map/all_gather | solution.py:73
  300.8 2.2 reshape.132
  302.9 2.8 fusion.54
  305.7 144.2 %all-gather.11.cloned.1.call-done = bf16[8192,256]{1,0:T(8,128)(2,1)} async-done(((bf16[128,256]{1,0:T(8,128)(2,1)}), bf16[8192,256]{1,0:T(8,128)(2,1)}) %all-gather.11.cloned.1.call-update) | async-done | bytes 4194320 | tf_op jit(solution)/shard_map/all_gather | solution.py:83
  449.9 6.3 copy.42
  456.2 138.1 %all-gather.9.cloned.1.call-done = bf16[8192,256]{0,1:T(8,128)(2,1)} async-done(((bf16[128,256]{0,1:T(8,128)(2,1)}), bf16[8192,256]{0,1:T(8,128)(2,1)}) %all-gather.9.cloned.1.call-update) | async-done | bytes 4194320 | tf_op jit(solution)/shard_map/all_gather | solution.py:82
  594.3 4.6 fusion.57
  599.0 0.2 fusion.28
  599.2 2.1 fusion.1
  601.4 2.5 fusion.15
  603.8 2.1 fusion.23
  605.9 1.8 convolution_convert_fusion
  607.8 43.7 %reduce-scatter.2.cloned.1.call-done = bf16[128,512]{1,0:T(8,128)(2,1)} async-done(((bf16[128,4096]{1,0:T(8,128)(2,1)}), bf16[128,512]{1,0:T(8,128)(2,1)}) %reduce-scatter.2.cloned.1.call-update) | async-done | bytes 131088 | tf_op jit(solution)/shard_map/reduce_scatter | solution.py:112
  651.5 1.0 multiply_reduce_fusion
  652.5 17.5 %psum.7 = f32[128]{0:T(128)S(1)} all-reduce(f32[128]{0:T(128)S(1)} %multiply_reduce_fusion), channel_id=1, replica_groups=mesh['ctx'=64,'dp'=8] {'dp'}, use_global_device_ids=true, to_apply=%region_7.8 | all-reduce | flops 128 | bytes 1024 | tf_op jit(solution)/shard_map/psum | solution.py:116
  670.0 1.7 multiply_convert_fusion
  (30 shorter events, 0.3 us)
Async XLA Ops:
  6.5 296.4 %copy-start = (bf16[2,4,128,128]{3,2,1,0:T(8,128)(2,1)S(1)}, bf16[2,4,128,128]{3,2,1,0:T(8,128)(2,1)}, u32[]{:S(2)}) copy-start(bf16[2,4,128,128]{3,2,1,0:T(8,128)(2,1)} %param.17) | copy-start | bytes 786436
  6.5 25.1 %copy-start.6 = (s32[2]{0:T(128)S(1)}, s32[2]{0:T(128)}, u32[]{:S(2)}) copy-start(s32[2]{0:T(128)} %param.22) | copy-start | bytes 28
  6.5 154.8 %all-gather.5.cloned.1.call-start = ((), (), s32[]{:S(2)}) async-start(), calls=%async_computation.2 | async-start | bytes 1064960 | tf_op jit(solution)/shard_map/all_gather | solution.py:72
  7.3 293.5 %all-gather.7.cloned.1.call-start = ((), (), s32[]{:S(2)}) async-start(), calls=%async_computation.3 | async-start | bytes 1064960 | tf_op jit(solution)/shard_map/all_gather | solution.py:73
  8.0 441.9 %all-gather.11.cloned.1.call-start = ((), (), s32[]{:S(2)}) async-start(), calls=%async_computation.5 | async-start | bytes 4259840 | tf_op jit(solution)/shard_map/all_gather | solution.py:83
  8.7 585.6 %all-gather.9.cloned.1.call-start = ((), (), s32[]{:S(2)}) async-start(), calls=%async_computation.4 | async-start | bytes 4259840 | tf_op jit(solution)/shard_map/all_gather | solution.py:82
  12.7 290.2 %copy-start.4 = (bf16[128,256]{1,0:T(8,128)(2,1)S(1)}, bf16[128,256]{1,0:T(8,128)(2,1)}, u32[]{:S(2)}) copy-start(bf16[128,256]{1,0:T(8,128)(2,1)} %param.12) | copy-start | bytes 196612
  12.7 593.2 %all-to-all-start = ((bf16[64,64,256]{2,1,0:T(8,128)(2,1)}), bf16[64,64,256]{2,1,0:T(8,128)(2,1)S(1)}, u32[]{:S(2)}, u32[]{:S(2)}) async-start(bf16[64,64,256]{2,1,0:T(8,128)(2,1)} %stack.2), calls=%async_computation | async-start | bytes 4194304 | tf_op jit(solution)/shard_map/all_to_all | solution.py:101
  31.6 619.9 %reduce-scatter.2.cloned.1.call-start = ((), (), s32[]{:S(2)}) async-start(), calls=%async_computation.6 | async-start | bytes 1179648 | tf_op jit(solution)/shard_map/reduce_scatter | solution.py:112
  594.3 4.7 copy-start.2
  599.2 2.2 copy-start.1
  603.8 3.9 copy-start.5
  603.8 47.7 %copy-start.3 = (bf16[128,512]{1,0:T(8,128)(2,1)S(1)}, bf16[128,512]{1,0:T(8,128)(2,1)}, u32[]{:S(2)}) copy-start(bf16[128,512]{1,0:T(8,128)(2,1)} %param.20) | copy-start | bytes 393220
Sparse Core Ops, SparseCore 0:
  10.6 150.6 all-gather.4
  164.6 136.1 all-gather.6
  304.1 145.7 all-gather.10
  452.7 141.5 all-gather.8
  607.9 43.5 reduce-scatter.1
